TPU v7x, 128 devices: a whole 4x4x4 slice. The times are simulated.
128 devices in a mesh: tm: 8 (over x, core), member: 16 (over z, y).
Axes of the slice: x: 4, y: 4, z: 4, core: 2. Of those that a mesh axis runs over, the one named last changes fastest.
Arguments:
- sensors: bfloat16 [16, 2048, 256], P('member', 'tm'), may hold values from -6 to 6
- kernel: bfloat16 [256, 256, 512], P('member'), may hold values from -0.0234375 to 0.0234375
- target: bfloat16 [16, 2048, 512], P('member', 'tm'), may hold values from -15 to 15
Outputs:
- errors: bfloat16 [16, 2048, 512], P('member', 'tm')
- whiteness: float32 [64, 512], replicated
All inputs are finite; a program needn't handle non-finite values.
Results may differ from a plain program's by a relative error of at most 0.0018.
Values may be sent and summed in bfloat16 or wider, within the bound.
No kernel may reach another device: no remote copies, remote signals or barrier semaphores. Data moves between devices by JAX's collectives and lax.ppermute only.
A program may use at most 64 MiB of HBM per device.

v0:
```python
import math
import jax
import jax.numpy as jnp
from jax import lax
from jax.sharding import PartitionSpec as P

LAGS = 64
EPS = 1e-06


def from_behind(shard, axis, by):
    peers = lax.axis_size(axis)
    pairs = [(i, i + by) for i in range(peers) if 0 <= i + by < peers]
    return lax.ppermute(shard, axis, pairs)


def shards(sensors, kernel, target):
    members_dev, steps_dev, channels = sensors.shape
    lag_dev = kernel.shape[0]
    kernel_span = lag_dev * lax.axis_size("member")
    first_lag = lax.axis_index("member") * lag_dev
    sensor_rim = from_behind(sensors, "tm", 1)
    joined = jnp.concatenate([sensor_rim, sensors], axis=1)
    gathered = lax.all_gather(joined, "member", axis=0, tiled=True)
    base = kernel_span - first_lag - (lag_dev - 1)

    def member_term(member_signal):
        block = lax.dynamic_slice_in_dim(member_signal, base, steps_dev + lag_dev - 1, 0)
        running = jnp.zeros((steps_dev, kernel.shape[2]), jnp.float32)
        for inner in range(lag_dev):
            window = block[lag_dev - 1 - inner : lag_dev - 1 - inner + steps_dev]
            running = running + jnp.dot(window, kernel[inner], preferred_element_type=jnp.float32)
        return running

    estimate = lax.psum_scatter(
        lax.map(member_term, gathered), "member", scatter_dimension=0, tiled=True
    )
    error_field = target.astype(jnp.float32) - estimate
    errors = error_field.astype(jnp.bfloat16)
    error_prior = from_behind(
        error_field[:, steps_dev - LAGS :, :].astype(jnp.bfloat16), "tm", 1
    ).astype(jnp.float32)
    joined_error = jnp.concatenate([error_prior, error_field], axis=1)

    def lag_sum(lag_index):
        window = lax.dynamic_slice_in_dim(joined_error, LAGS - lag_index, steps_dev, 1)
        return jnp.sum(error_field * window, axis=(0, 1))

    lag_partial = lax.map(lag_sum, jnp.arange(LAGS + 1, dtype=jnp.int32))
    totals = lax.psum(lag_partial, ("tm", "member"))
    sample_count = float(members_dev * lax.axis_size("member") * steps_dev * lax.axis_size("tm"))
    whiteness = (
        math.sqrt(sample_count) * (totals[1:] / sample_count) / (totals[0] / sample_count + EPS)
    )
    return (errors, whiteness)


def solution(mesh):
    in_specs = (P("member", "tm", None), P("member", None, None), P("member", "tm", None))
    out_specs = (P("member", "tm", None), P())
    return jax.shard_map(shards, mesh=mesh, in_specs=in_specs, out_specs=out_specs, check_vma=False)
```

profile of v0, /device:TPU:1, one launch (start us, length us, event | category | flops | bytes accessed | tf_op | source)
XLA Modules:
  0.0 877.6 jit_solution(1692239495963471276)
XLA Ops:
  7.2 4.5 collective-permute-start
  11.7 2.2 collective-permute-done
  14.0 1.6 pad_maximum_fusion.1
  15.7 54.4 %all-gather.2.cloned.1.call-done = bf16[16,512,256]{2,1,0:T(8,128)(2,1)} async-done(((bf16[1,512,256]{2,1,0:T(8,128)(2,1)}), bf16[16,512,256]{2,1,0:T(8,128)(2,1)}) %all-gather.2.cloned.1.call-update) | async-done | bytes 4194320 | tf_op jit(solution)/shard_map/all_gather | solution.py:24
  70.1 339.0 %while.25 = (s32[]{:T(128)}, f32[16,256,512]{2,1,0:T(8,128)}, bf16[16,512,256]{2,1,0:T(8,128)(2,1)}, s32[]{:T(128)}, bf16[16,256,512]{2,1,0:T(8,128)(2,1)}, /*in...) while((s32[]{:T(128)}, f32[16,256,512]{2,1,0:T(8,128)}, ...), condition=%wide.region_1.2_spmd, body=%wide.region_0.1_spmd.sunk | while | flops 1075707904 | bytes 22545932 | solution.py:36
  89.2 2.1 fusion.89
  110.3 2.1 fusion.89
  131.5 2.1 fusion.89
  152.7 2.1 fusion.89
  173.9 2.1 fusion.89
  195.1 2.1 fusion.89
  216.3 2.1 fusion.89
  237.4 2.1 fusion.89
  258.6 2.1 fusion.89
  279.8 2.1 fusion.89
  301.0 2.1 fusion.89
  322.2 2.1 fusion.89
  343.4 2.1 fusion.89
  364.6 2.1 fusion.89
  385.7 2.1 fusion.89
  406.9 2.1 fusion.89
  409.1 84.6 %reduce-scatter.4.cloned.1.call-done = f32[1,256,512]{2,1,0:T(8,128)} async-done(((f32[16,256,512]{2,1,0:T(8,128)}), f32[1,256,512]{2,1,0:T(8,128)}) %reduce-scatter.4.cloned.1.call-update) | async-done | bytes 524304
  494.9 5.1 collective-permute-start.1
  501.4 225.3 %while.26 = (s32[]{:T(128)}, f32[65,512]{1,0:T(8,128)}, s32[65]{0:T(128)S(1)}, f32[1,320,512]{2,1,0:T(8,128)S(1)}, f32[1,256,512]{2,1,0:T(8,128)S(1)}, /*index=5*/s32[]{:T(128)}, s32[1]{0:T(128)}, s32[]{:T(128)}, s32[1]{0:T(128)}) while((s32[]{:T(128)}, f32[65,512]{1,0:T(8,128)}, s32[65]{0:T(128)S(1)}, f32[1,320,512]{2,1,0:T(8,128)S(1)}, ...), condition=%wide.region_5.6_spmd, body=%wide.region_3.5_spmd.sunk | while | flops 261638 | bytes 1054879 | solution.py:49
  531.2 1.3 dynamic_update_slice.19
  534.7 1.3 dynamic_update_slice.19
  538.2 1.3 dynamic_update_slice.19
  541.6 1.3 dynamic_update_slice.19
  545.1 1.3 dynamic_update_slice.19
  548.6 1.3 dynamic_update_slice.19
  552.0 1.3 dynamic_update_slice.19
  555.5 1.3 dynamic_update_slice.19
  559.0 1.3 dynamic_update_slice.19
  562.4 1.3 dynamic_update_slice.19
  565.9 1.3 dynamic_update_slice.19
  569.4 1.3 dynamic_update_slice.19
  572.8 1.3 dynamic_update_slice.19
  579.8 1.3 dynamic_update_slice.19
  642.1 1.3 dynamic_update_slice.19
  645.6 1.3 dynamic_update_slice.19
  649.1 1.3 dynamic_update_slice.19
  652.6 1.3 dynamic_update_slice.19
  656.0 1.3 dynamic_update_slice.19
  659.5 1.3 dynamic_update_slice.19
  663.0 1.3 dynamic_update_slice.19
  666.4 1.3 dynamic_update_slice.19
  726.7 142.1 %all-reduce.3.cloned.1.call-done = f32[65,512]{1,0:T(8,128)} async-done(((f32[65,512]{1,0:T(8,128)}), f32[65,512]{1,0:T(8,128)}) %all-reduce.3.cloned.1.call-update) | async-done | bytes 133136 | tf_op jit(solution)/shard_map/psum | solution.py:50
  869.5 1.6 fusion.51
  (432 shorter events, 413.3 us)
Async XLA Ops:
  7.2 62.9 %all-gather.2.cloned.1.call-start = ((), (), s32[]{:S(2)}) async-start(), calls=%async_computation.1 | async-start | bytes 4456448 | tf_op jit(solution)/shard_map/all_gather | solution.py:24
  7.2 6.7 collective-permute-start
  15.6 478.1 %reduce-scatter.4.cloned.1.call-start = ((), (), s32[]{:S(2)}) async-start(), calls=%async_computation.3 | async-start | bytes 8912896
  409.0 84.7 %copy-start.1 = (bf16[1,256,512]{2,1,0:T(8,128)(2,1)S(1)}, bf16[1,256,512]{2,1,0:T(8,128)(2,1)}, u32[]{:S(2)}) copy-start(bf16[1,256,512]{2,1,0:T(8,128)(2,1)} %param.9) | copy-start | bytes 786436
  409.0 459.7 %all-reduce.3.cloned.1.call-start = ((), (), s32[]{:S(2)}) async-start(), calls=%async_computation.2 | async-start | bytes 294912 | tf_op jit(solution)/shard_map/psum | solution.py:50
  494.8 376.2 %copy-start = (bf16[1,256,512]{2,1,0:T(8,128)(2,1)}, bf16[1,256,512]{2,1,0:T(8,128)(2,1)S(1)}, u32[]{:S(2)}) copy-start(bf16[1,256,512]{2,1,0:T(8,128)(2,1)S(1)} %get-tuple-element.186) | copy-start | bytes 786436
  494.9 6.4 collective-permute-start.1
Sparse Core Ops, SparseCore 0:
  15.7 54.2 all-gather.1
  409.2 84.5 reduce-scatter.3
  726.8 141.8 all-reduce.2
where the time goes:
time: 888 us; the launch traced here: 878 us
  matrix products  336 us (38%)
  waiting for transfers between devices  285 us (32%)
  local copies, waits for them, and re-layouts  129 us (15%)
  loops' own time  91.8 us (10%)
  between operations  13.8 us (2%)
  other arithmetic  12.2 us (1%)
  starting transfers between devices  9.73 us (1%)
    dot_general x256, matrix products, member_term(): jnp.dot(window, kernel[inner], preferred_element_type=jnp.float32)  336 us
    psum x1, waiting for transfers between devices, shards(): totals = lax.psum(lag_partial, ('tm', 'member'))  142 us
    another operation x1, loops' own time, shards(): lag_partial = lax.map(lag_sum, jnp.arange(LAGS + 1, dtype=jnp.int32))  89.2 us
    dynamic_update_slice x65, local copies, waits for them, and re-layouts, shards(): lag_partial = lax.map(lag_sum, jnp.arange(LAGS + 1, dtype=jnp.int32))  86.7 us
    unnamed x4, waiting for transfers between devices  84.7 us
    all_gather x1, waiting for transfers between devices, shards(): gathered = lax.all_gather(joined, 'member', axis=0, tiled=True)  54.4 us
    dynamic_slice x65, local copies, waits for them, and re-layouts, shards(): lag_partial = lax.map(lag_sum, jnp.arange(LAGS + 1, dtype=jnp.int32))  42.3 us
  transfers between devices with their start and end apart: 5, of which 5 were waited for; matrix products, arithmetic and copies ran while one was open for 0% of the time, Pallas kernels for 0%

commit v1 on v0

--- a/solution.py
+++ b/solution.py
@@ -47,7 +47,7 @@
         return jnp.sum(error_field * window, axis=(0, 1))
 
     lag_partial = lax.map(lag_sum, jnp.arange(LAGS + 1, dtype=jnp.int32))
-    totals = lax.psum(lag_partial, ("tm", "member"))
+    totals = jnp.sum(lax.all_gather(lag_partial, ("tm", "member")), axis=0)
     sample_count = float(members_dev * lax.axis_size("member") * steps_dev * lax.axis_size("tm"))
     whiteness = (
         math.sqrt(sample_count) * (totals[1:] / sample_count) / (totals[0] / sample_count + EPS)

time: 888 us -> 836 us (0.941)
  waiting for transfers between devices: 285 us -> 226 us
    psum x1 -> x0, waiting for transfers between devices: 142 us -> none  [shards(): totals = lax.psum(lag_partial, ('tm', 'member'))]
    all_gather x0 -> x1, waiting for transfers between devices: none -> 83.4 us  [shards(): totals = jnp.sum(lax.all_gather(lag_partial, ('tm', 'member')), axis=0)]
where the time goes in v1:
time: 836 us; the launch traced here: 825 us
  matrix products  336 us (40%)
  waiting for transfers between devices  226 us (27%)
  local copies, waits for them, and re-layouts  129 us (15%)
  loops' own time  91.8 us (11%)
  other arithmetic  18.7 us (2%)
  between operations  13.8 us (2%)
  starting transfers between devices  9.73 us (1%)
    dot_general x256, matrix products, member_term(): jnp.dot(window, kernel[inner], preferred_element_type=jnp.float32)  336 us
    another operation x1, loops' own time, shards(): lag_partial = lax.map(lag_sum, jnp.arange(LAGS + 1, dtype=jnp.int32))  89.2 us
    dynamic_update_slice x65, local copies, waits for them, and re-layouts, shards(): lag_partial = lax.map(lag_sum, jnp.arange(LAGS + 1, dtype=jnp.int32))  86.7 us
    unnamed x4, waiting for transfers between devices  84.7 us
    all_gather x1, waiting for transfers between devices, shards(): totals = jnp.sum(lax.all_gather(lag_partial, ('tm', 'member')), axis=0)  83.4 us
    all_gather x1, waiting for transfers between devices, shards(): gathered = lax.all_gather(joined, 'member', axis=0, tiled=True)  54.4 us
    dynamic_slice x65, local copies, waits for them, and re-layouts, shards(): lag_partial = lax.map(lag_sum, jnp.arange(LAGS + 1, dtype=jnp.int32))  42.3 us
  transfers between devices with their start and end apart: 5, of which 5 were waited for; matrix products, arithmetic and copies ran while one was open for 0% of the time, Pallas kernels for 0%

profile of v1, /device:TPU:1, one launch (start us, length us, event | category | flops | bytes accessed | tf_op | source)
XLA Modules:
  0.0 825.4 jit_solution(10836154203207526199)
XLA Ops:
  7.2 4.5 collective-permute-start
  11.7 2.2 collective-permute-done
  14.0 1.6 pad_maximum_fusion.1
  15.7 54.4 %all-gather.5.cloned.1.call-done = bf16[16,512,256]{2,1,0:T(8,128)(2,1)} async-done(((bf16[1,512,256]{2,1,0:T(8,128)(2,1)}), bf16[16,512,256]{2,1,0:T(8,128)(2,1)}) %all-gather.5.cloned.1.call-update) | async-done | bytes 4194320 | tf_op jit(solution)/shard_map/all_gather | solution.py:24
  70.1 339.0 %while.25 = (s32[]{:T(128)}, f32[16,256,512]{2,1,0:T(8,128)}, bf16[16,512,256]{2,1,0:T(8,128)(2,1)}, s32[]{:T(128)}, bf16[16,256,512]{2,1,0:T(8,128)(2,1)}, /*in...) while((s32[]{:T(128)}, f32[16,256,512]{2,1,0:T(8,128)}, ...), condition=%wide.region_1.2_spmd, body=%wide.region_0.1_spmd.sunk | while | flops 1075707904 | bytes 22545932 | solution.py:36
  89.2 2.1 fusion.89
  110.3 2.1 fusion.89
  131.5 2.1 fusion.89
  152.7 2.1 fusion.89
  173.9 2.1 fusion.89
  195.1 2.1 fusion.89
  216.3 2.1 fusion.89
  237.4 2.1 fusion.89
  258.6 2.1 fusion.89
  279.8 2.1 fusion.89
  301.0 2.1 fusion.89
  322.2 2.1 fusion.89
  343.4 2.1 fusion.89
  364.6 2.1 fusion.89
  385.7 2.1 fusion.89
  406.9 2.1 fusion.89
  409.1 84.6 %reduce-scatter.4.cloned.1.call-done = f32[1,256,512]{2,1,0:T(8,128)} async-done(((f32[16,256,512]{2,1,0:T(8,128)}), f32[1,256,512]{2,1,0:T(8,128)}) %reduce-scatter.4.cloned.1.call-update) | async-done | bytes 524304
  494.9 5.1 collective-permute-start.1
  501.4 225.2 %while.26 = (s32[]{:T(128)}, f32[65,512]{1,0:T(8,128)}, s32[65]{0:T(128)S(1)}, f32[1,320,512]{2,1,0:T(8,128)S(1)}, f32[1,256,512]{2,1,0:T(8,128)S(1)}, /*index=5*/s32[]{:T(128)}, s32[1]{0:T(128)}, s32[]{:T(128)}, s32[1]{0:T(128)}) while((s32[]{:T(128)}, f32[65,512]{1,0:T(8,128)}, s32[65]{0:T(128)S(1)}, f32[1,320,512]{2,1,0:T(8,128)S(1)}, ...), condition=%wide.region_5.6_spmd, body=%wide.region_3.5_spmd.sunk | while | flops 261638 | bytes 1054879 | solution.py:49
  531.2 1.3 dynamic_update_slice.19
  534.7 1.3 dynamic_update_slice.19
  538.2 1.3 dynamic_update_slice.19
  541.6 1.3 dynamic_update_slice.19
  545.1 1.3 dynamic_update_slice.19
  548.6 1.3 dynamic_update_slice.19
  586.7 1.3 dynamic_update_slice.19
  590.2 1.3 dynamic_update_slice.19
  593.6 1.3 dynamic_update_slice.19
  597.1 1.3 dynamic_update_slice.19
  600.5 1.3 dynamic_update_slice.19
  604.0 1.3 dynamic_update_slice.19
  607.5 1.3 dynamic_update_slice.19
  610.9 1.3 dynamic_update_slice.19
  669.8 1.3 dynamic_update_slice.19
  673.3 1.3 dynamic_update_slice.19
  676.8 1.3 dynamic_update_slice.19
  680.2 1.3 dynamic_update_slice.19
  683.7 1.3 dynamic_update_slice.19
  687.2 1.3 dynamic_update_slice.19
  690.6 1.3 dynamic_update_slice.19
  694.1 1.3 dynamic_update_slice.19
  726.6 83.4 %all-gather.7.cloned.1.call-done = f32[128,65,512]{2,1,0:T(8,128)} async-done(((f32[1,65,512]{2,1,0:T(8,128)}), f32[128,65,512]{2,1,0:T(8,128)}) %all-gather.7.cloned.1.call-update) | async-done | bytes 17039376 | tf_op jit(solution)/shard_map/all_gather | solution.py:50
  810.1 8.1 reduce_sum.21
  (433 shorter events, 413.3 us)
Async XLA Ops:
  7.2 62.9 %all-gather.5.cloned.1.call-start = ((), (), s32[]{:S(2)}) async-start(), calls=%async_computation.1 | async-start | bytes 4456448 | tf_op jit(solution)/shard_map/all_gather | solution.py:24
  7.2 6.7 collective-permute-start
  15.6 478.1 %reduce-scatter.4.cloned.1.call-start = ((), (), s32[]{:S(2)}) async-start(), calls=%async_computation.3 | async-start | bytes 8912896
  409.0 84.7 %copy-start.1 = (bf16[1,256,512]{2,1,0:T(8,128)(2,1)S(1)}, bf16[1,256,512]{2,1,0:T(8,128)(2,1)}, u32[]{:S(2)}) copy-start(bf16[1,256,512]{2,1,0:T(8,128)(2,1)} %param.9) | copy-start | bytes 786436
  409.0 401.0 %all-gather.7.cloned.1.call-start = ((), (), s32[]{:S(2)}) async-start(), calls=%async_computation.2 | async-start | bytes 19021824 | tf_op jit(solution)/shard_map/all_gather | solution.py:50
  494.8 323.3 %copy-start = (bf16[1,256,512]{2,1,0:T(8,128)(2,1)}, bf16[1,256,512]{2,1,0:T(8,128)(2,1)S(1)}, u32[]{:S(2)}) copy-start(bf16[1,256,512]{2,1,0:T(8,128)(2,1)S(1)} %get-tuple-element.186) | copy-start | bytes 786436
  494.9 6.4 collective-permute-start.1
Sparse Core Ops, SparseCore 0:
  15.7 54.2 all-gather.4
  409.2 84.5 reduce-scatter.3
  726.8 83.2 all-gather.6
